TPU v7x, 256 devices: a whole 4x4x8 slice. The times are simulated.
256 devices in a mesh: rep: 4 (over x), shard: 32 (over y, z_lo, core), tp: 2 (over z_hi).
Axes of the slice: x: 4, y: 4, z: 8 (z_hi: 2, z_lo: 4; z = z_hi * 4 + z_lo), core: 2. Of those that a mesh axis runs over, the one named last changes fastest.
Arguments:
- qkv_delta: float32 [4, 4, 1024, 3, 1024], P('rep', None, 'shard', None, 'tp'), may hold values from -6 to 6
- wi_delta: float32 [4, 4, 1024, 2, 2816], P('rep', None, 'shard', None, 'tp'), may hold values from -6 to 6
- basis: float32 [1024, 64], replicated, may hold values from -0.1875 to 0.1875
- qkv_master: float32 [2, 4, 3, 512, 1024], P('tp', None, None, ('rep', 'shard')), may hold values from -6 to 6
- qkv_momentum: float32 [2, 4, 3, 512, 1024], P('tp', None, None, ('rep', 'shard')), may hold values from -6 to 6
- wi_master: float32 [2, 4, 2, 1408, 1024], P('tp', None, None, ('rep', 'shard')), may hold values from -6 to 6
- wi_momentum: float32 [2, 4, 2, 1408, 1024], P('tp', None, None, ('rep', 'shard')), may hold values from -6 to 6
Outputs:
- qkv_master_new: float32 [2, 4, 3, 512, 1024], P('tp', None, None, ('rep', 'shard'))
- qkv_momentum_new: float32 [2, 4, 3, 512, 1024], P('tp', None, None, ('rep', 'shard'))
- wi_master_new: float32 [2, 4, 2, 1408, 1024], P('tp', None, None, ('rep', 'shard'))
- wi_momentum_new: float32 [2, 4, 2, 1408, 1024], P('tp', None, None, ('rep', 'shard'))
- qkv_train: float32 [4, 1024, 3, 1024], P(None, 'shard', None, 'tp')
- wi_train: float32 [4, 1024, 2, 2816], P(None, 'shard', None, 'tp')
All inputs are finite; a program needn't handle non-finite values.
Results may differ from a plain program's by a relative error of at most 0.00007.
Values sent between devices are 32-bit elements; how exact they have to be, the bound alone decides.
A program may use at most 64 MiB of HBM per device.

v0:
```python
import jax
import jax.numpy as jnp
from jax import lax
from jax.sharding import PartitionSpec as P


def outer_update(master, momentum, average):
    momentum_new = 0.9 * momentum + average[None]
    master_new = master - 0.7 * (average[None] + 0.9 * momentum_new)
    return (master_new, momentum_new)


def to_wire(local, replicas, shards):
    layers, width_local, groups, cols = local.shape
    share = cols // (replicas * shards)
    shaped = local.reshape(layers, width_local, groups, replicas, shards, share)
    shaped = jnp.transpose(shaped, (0, 2, 3, 4, 5, 1))
    return shaped.reshape(layers, groups, replicas, shards, share * width_local)


def to_owner(moved, width_local):
    layers, groups, shards = (moved.shape[0], moved.shape[1], moved.shape[3])
    share = moved.shape[4] // width_local
    shaped = moved.reshape(layers, groups, shards, share, width_local)
    shaped = jnp.transpose(shaped, (0, 1, 3, 2, 4))
    return shaped.reshape(layers, groups, share, shards * width_local)


def to_block(owner, shards):
    layers, groups, share, width = owner.shape
    width_local = width // shards
    shaped = owner.reshape(layers, groups, share, shards, width_local)
    shaped = jnp.transpose(shaped, (0, 1, 3, 2, 4))
    return shaped.reshape(layers, groups, 1, shards, share * width_local)


def to_train(spread, width_local):
    layers, groups, replicas, shards = (
        spread.shape[0],
        spread.shape[1],
        spread.shape[2],
        spread.shape[3],
    )
    share = spread.shape[4] // width_local
    shaped = spread.reshape(layers, groups, replicas, shards, share, width_local)
    shaped = jnp.transpose(shaped, (0, 5, 1, 2, 3, 4))
    return shaped.reshape(layers, width_local, groups, replicas * shards * share)


def per_device(qkv_delta, wi_delta, basis, qkv_master, qkv_momentum, wi_master, wi_momentum):
    replicas = lax.axis_size("rep")
    shards = lax.axis_size("shard")
    width_local = qkv_delta.shape[2]
    qkv_local = to_wire(qkv_delta[0], replicas, shards)
    summed = lax.psum_scatter(qkv_local, "rep", scatter_dimension=2, tiled=True)
    moved = lax.all_to_all(summed, "shard", split_axis=3, concat_axis=3, tiled=True)
    qkv_avg = to_owner(moved, width_local) / replicas
    basis_rows = lax.dynamic_slice_in_dim(
        basis, lax.axis_index("shard") * width_local, width_local, 0
    )
    partial_value = jnp.einsum(
        "ldgf,dk->lgfk", wi_delta[0], basis_rows, precision=lax.Precision.HIGHEST
    )
    coef = (
        lax.psum_scatter(partial_value, ("rep", "shard"), scatter_dimension=2, tiled=True)
        / replicas
    )
    wi_avg = jnp.einsum("lgck,dk->lgcd", coef, basis, precision=lax.Precision.HIGHEST)
    qkv_master_new, qkv_momentum_new = outer_update(qkv_master, qkv_momentum, qkv_avg)
    wi_master_new, wi_momentum_new = outer_update(wi_master, wi_momentum, wi_avg)
    qkv_block = to_block(qkv_master_new[0], shards)
    wi_block = to_block(wi_master_new[0], shards)
    qkv_stacked, wi_stacked = (
        lax.all_gather(qkv_block, "rep", axis=2, tiled=True),
        lax.all_gather(wi_block, "rep", axis=2, tiled=True),
    )
    qkv_spread, wi_spread = (
        lax.all_to_all(qkv_stacked, "shard", split_axis=3, concat_axis=3, tiled=True),
        lax.all_to_all(wi_stacked, "shard", split_axis=3, concat_axis=3, tiled=True),
    )
    return (
        qkv_master_new,
        qkv_momentum_new,
        wi_master_new,
        wi_momentum_new,
        to_train(qkv_spread, width_local),
        to_train(wi_spread, width_local),
    )


def solution(mesh):
    in_specs = (
        P("rep", None, "shard", None, "tp"),
        P("rep", None, "shard", None, "tp"),
        P(),
        P("tp", None, None, ("rep", "shard"), None),
        P("tp", None, None, ("rep", "shard"), None),
        P("tp", None, None, ("rep", "shard"), None),
        P("tp", None, None, ("rep", "shard"), None),
    )
    out_specs = (
        P("tp", None, None, ("rep", "shard"), None),
        P("tp", None, None, ("rep", "shard"), None),
        P("tp", None, None, ("rep", "shard"), None),
        P("tp", None, None, ("rep", "shard"), None),
        P(None, "shard", None, "tp"),
        P(None, "shard", None, "tp"),
    )
    return jax.shard_map(
        per_device, mesh=mesh, in_specs=in_specs, out_specs=out_specs, check_vma=False
    )
```

profile of v0, /device:TPU:1, one launch (start us, length us, event | category | flops | bytes accessed | tf_op | source)
XLA Modules:
  0.0 1510.4 jit_solution(9383399998009332308)
XLA Ops:
  7.2 0.0 copy-start
  7.2 0.0 all-reduce.5.cloned.1.call-start
  7.2 3.2 copy.91
  10.4 3.6 reshape.49
  14.1 0.0 all-reduce.5.cloned.1.call-update
  14.1 0.0 all-reduce.7.cloned.1.call-start
  14.1 0.0 copy-done
  14.1 0.0 copy-done.7
  14.1 4.1 convolution_bitcast_fusion
  18.2 6.3 copy.97
  24.6 0.0 all-reduce.7.cloned.1.call-update
  24.6 0.0 copy-start.5
  24.6 0.0 copy-start.6
  24.6 0.6 copy-done.11
  25.2 0.6 dynamic-slice.2
  25.8 0.0 copy-done.10
  25.8 0.6 dynamic-slice
  27.1 38.6 %all-reduce.5.cloned.1.call-done = f32[4,3,4,32,128]{4,3,2,1,0:T(8,128)} async-done(((f32[4,3,4,32,128]{4,3,2,1,0:T(8,128)}), f32[4,3,4,32,128]{4,3,2,1,0:T(8,128)}) %all-reduce.5.cloned.1.call-update) | async-done | bytes 786448
  65.7 1.6 constant_dynamic-slice_fusion
  67.3 0.9 copy.92
  68.2 9.9 all-to-all-start
  78.1 0.0 all-gather.2.cloned.1.call-start
  78.1 1296.3 %all-reduce.7.cloned.1.call-done = f32[4,2,1408,64]{3,0,1,2:T(4,128)} async-done(((f32[4,2,1408,64]{3,0,1,2:T(4,128)}), f32[4,2,1408,64]{3,0,1,2:T(4,128)}) %all-reduce.7.cloned.1.call-update) | async-done | bytes 2883600
  1374.4 0.8 dynamic-slice_multiply_fusion
  1375.2 0.0 copy-done.5
  1375.2 0.0 copy-done.6
  1375.2 1.6 fusion.1
  1376.8 0.3 copy.109
  1377.1 0.0 copy-start.3
  1377.1 1.7 reshape_squeeze.11
  1378.9 2.2 copy.105
  1381.1 1.3 reshape.53
  1382.4 0.0 all-gather.2.cloned.1.call-update
  1382.4 0.0 all-to-all-done
  1382.4 0.9 copy_multiply_fusion.1
  1383.4 0.0 copy-start.8
  1383.4 0.0 copy-start.9
  1383.4 0.3 div.20
  1383.7 0.1 copy.94
  1383.8 0.4 div.22
  1384.2 0.1 copy-done.8
  1384.3 0.1 copy-done.9
  1384.4 0.8 multiply_subtract_fusion
  1385.2 0.7 copy-done.4
  1385.9 0.3 reshape_squeeze.10
  1386.1 0.5 copy.132
  1386.7 0.4 reshape.50
  1387.0 13.5 all_gather.6
  1400.6 1.4 copy.102
  1402.0 8.8 all-to-all-start.1
  1410.8 2.3 all-gather.2.cloned.1.call-done
  1413.2 3.8 copy.106
  1416.9 16.3 %all-to-all-done.1 = f32[4,3,4,32,128]{4,2,1,0,3:T(4,128)S(1)} async-done(((f32[4,3,4,32,128]{4,2,1,0,3:T(4,128)}), f32[4,3,4,32,128]{4,2,1,0,3:T(4,128)S(1)}, u32[]{:S(2)}, u32[]{:S(2)}) %all-to-all-start.1) | async-done | bytes 786464 | tf_op jit(solution)/shard_map/all_to_all | solution.py:78
  1433.2 0.9 copy-done.1
  1434.1 3.9 all-to-all-start.2
  1438.0 2.3 copy.103
  1440.3 3.6 reshape.51
  1443.9 3.1 copy.111
  1447.0 1.0 copy.110
  1448.0 29.0 %all-to-all-done.2 = f32[4,2,4,32,352]{4,1,0,2,3:T(2,128)S(1)} async-done(((f32[4,2,4,32,352]{4,1,0,2,3:T(2,128)}), f32[4,2,4,32,352]{4,1,0,2,3:T(2,128)S(1)}, u32[]{:S(2)}, u32[]{:S(2)}) %all-to-all-start.2) | async-done | bytes 1441824 | tf_op jit(solution)/shard_map/all_to_all | solution.py:79
  1477.0 2.1 copy.107
  1479.1 6.0 reshape.54
  1485.1 10.4 copy.108
  1495.5 8.4 copy.112
  (8 shorter events, 0.0 us)
Async XLA Ops:
  7.2 7.0 copy-start
  7.2 58.5 %all-reduce.5.cloned.1.call-start = ((), (), s32[]{:S(2)}) async-start(), calls=%async_computation.4 | async-start | bytes 1572864
  10.4 3.7 copy-start.7
  14.1 1360.4 %all-reduce.7.cloned.1.call-start = ((), (), s32[]{:S(2)}) async-start(), calls=%async_computation.5 | async-start | bytes 11534336
  24.6 0.7 copy-start.11
  24.6 1.3 copy-start.10
  24.6 1350.6 %copy-start.5 = (f32[1,4,2,11,1024]{4,2,3,1,0:T(2,128)S(1)}, f32[1,4,2,11,1024]{4,2,3,1,0:T(2,128)}, u32[]{:S(2)}) copy-start(f32[1,4,2,11,1024]{4,2,3,1,0:T(2,128)} %param.13) | copy-start | bytes 1081348
  24.6 1350.6 %copy-start.6 = (f32[1,4,2,11,1024]{4,2,3,1,0:T(2,128)S(1)}, f32[1,4,2,11,1024]{4,2,3,1,0:T(2,128)}, u32[]{:S(2)}) copy-start(f32[1,4,2,11,1024]{4,2,3,1,0:T(2,128)} %param.12) | copy-start | bytes 1081348
  68.2 1314.2 %all-to-all-start = ((f32[4,3,1,32,128]{4,2,1,0,3:T(1,128)}), f32[4,3,1,32,128]{4,2,1,0,3:T(1,128)}, u32[]{:S(2)}, u32[]{:S(2)}) async-start(f32[4,3,1,32,128]{4,2,1,0,3:T(1,128)} %copy.92), calls=%async_computation | async-start | bytes 393216 | tf_op jit(solution)/shard_map/all_to_all | solution.py:56
  78.1 1335.1 %all-gather.2.cloned.1.call-start = ((), (), s32[]{:S(2)}) async-start(), calls=%async_computation.3 | async-start | bytes 1966080 | tf_op jit(solution)/shard_map/all_gather | solution.py:75
  1377.1 1.7 copy-start.3
  1383.4 0.9 copy-start.8
  1383.4 1.0 copy-start.9
  1385.2 0.7 copy-start.4
  1402.0 31.3 %all-to-all-start.1 = ((f32[4,3,4,32,128]{4,2,1,0,3:T(4,128)}), f32[4,3,4,32,128]{4,2,1,0,3:T(4,128)S(1)}, u32[]{:S(2)}, u32[]{:S(2)}) async-start(f32[4,3,4,32,128]{4,2,1,0,3:T(4,128)} %copy.102), calls=%async_computation.1 | async-start | bytes 1572864 | tf_op jit(solution)/shard_map/all_to_all | solution.py:78
  1433.2 0.9 copy-start.1
  1434.1 42.9 %all-to-all-start.2 = ((f32[4,2,4,32,352]{4,1,0,2,3:T(2,128)}), f32[4,2,4,32,352]{4,1,0,2,3:T(2,128)S(1)}, u32[]{:S(2)}, u32[]{:S(2)}) async-start(f32[4,2,4,32,352]{4,1,0,2,3:T(2,128)} %copy.106), calls=%async_computation.2 | async-start | bytes 3145728 | tf_op jit(solution)/shard_map/all_to_all | solution.py:79
  1443.9 3.1 copy-start.2
Sparse Core Ops, SparseCore 0:
  14.2 51.4 all-reduce.4
  68.3 1306.0 all-reduce.6
  1382.5 30.5 all-gather.1
where the time goes:
time: 1510 us
  waiting for transfers between devices  1380 us (91%)
  local copies, waits for them, and re-layouts  68.7 us (5%)
  starting transfers between devices  22.7 us (2%)
    unnamed x5, waiting for transfers between devices  1330 us
  transfers between devices with their start and end apart: 6, of which 5 were waited for; matrix products, arithmetic and copies ran while one was open for 3% of the time, Pallas kernels for 0%

commit v1 on v0

v1 whole, which is shorter than its diff:
```python
import functools

import jax
import jax.numpy as jnp
from jax import lax
from jax.experimental import pallas as pl
from jax.experimental.pallas import tpu as pltpu
from jax.sharding import PartitionSpec as P

LANES = 128


def swap_blocks(four, masks):
    low_half, even = masks
    a, b, c, d = four
    a, c = jnp.where(low_half, a, pltpu.roll(c, 64, 1)), jnp.where(low_half, pltpu.roll(a, 64, 1), c)
    b, d = jnp.where(low_half, b, pltpu.roll(d, 64, 1)), jnp.where(low_half, pltpu.roll(b, 64, 1), d)
    a, b = jnp.where(even, a, pltpu.roll(b, 32, 1)), jnp.where(even, pltpu.roll(a, 96, 1), b)
    c, d = jnp.where(even, c, pltpu.roll(d, 32, 1)), jnp.where(even, pltpu.roll(c, 96, 1), d)
    return a, b, c, d


def block_masks(rows):
    lane = lax.broadcasted_iota(jnp.int32, (rows, LANES), 1)
    return lane < 64, lax.rem(lax.div(lane, 32), 2) == 0


def outer_update(master, momentum, average):
    momentum_new = 0.9 * momentum + average
    return master - 0.7 * (average + 0.9 * momentum_new), momentum_new


def kernel(reps, shards, *refs):
    (qkv_in, wi_in, basis_in, qm_in, qv_in, wm_in, wv_in,
     qm_out, qv_out, wm_out, wv_out, qt_out, wt_out,
     xq, xw, w, far_q, direct_q, joined_q, partial_q, far_w, direct_w, joined_w, partial_w, send, got, back, gq, yq, gw, yw,
     dq, dw, aw, basis, qm, qv, wm, wv,
     rs_send, rs_recv, ag_send, ag_recv, fw_send, fw_recv, bw_send, bw_recv,
     in_sem, out_sem) = refs
    layers, groups, width, block = xq.shape[1:]
    share_q, share_w = qm.shape[2], wm.shape[2]
    me = lax.axis_index("rep")
    own = lax.axis_index("shard")
    after = lax.rem(me + 1, reps)
    before = lax.rem(me + reps - 1, reps)
    across = lax.rem(me + 2, reps)
    quads = shards // 4
    share = (groups * share_q, share_w, share_w)
    rows = tuple(shards * n for n in share)
    half = tuple(n // 2 for n in rows)
    chunks = range(3)

    loads = [pltpu.make_async_copy(qkv_in.at[:, :, :, pl.ds(j * block, block)], xq.at[j], in_sem.at[10 + j])
             for j in range(reps)]
    wi_loads = [pltpu.make_async_copy(wi_in.at[:, :, g, :], xw.at[g], in_sem.at[1 + g]) for g in range(2)]
    state_loads = [pltpu.make_async_copy(qm_in, qm, in_sem.at[3]), pltpu.make_async_copy(qv_in, qv, in_sem.at[4]),
                   pltpu.make_async_copy(basis_in, basis, in_sem.at[5])]
    for g in range(2):
        state_loads += [pltpu.make_async_copy(wm_in.at[:, :, g, :], wm.at[g], in_sem.at[6 + g]),
                        pltpu.make_async_copy(wv_in.at[:, :, g, :], wv.at[g], in_sem.at[8 + g])]
    for copy in loads + wi_loads + state_loads:
        copy.start()

    barrier = pltpu.get_barrier_semaphore()
    for target in (after, before):
        pl.semaphore_signal(barrier, inc=1, device_id={"rep": target})

    def greet(j, carry):
        pl.semaphore_signal(barrier, inc=1, device_id={"shard": lax.rem(own + j, shards)})
        return carry

    lax.fori_loop(1, shards, greet, 0)
    dw[...] = jnp.zeros_like(dw)
    pl.semaphore_wait(barrier, shards + 1)

    def half_of(k, slot, part, q_ref, w_ref):
        if k == 0:
            return q_ref.at[slot, pl.ds(part * (layers // 2), layers // 2)]
        return w_ref.at[k - 1, pl.ds(pl.multiple_of(slot * rows[k] + part * half[k], 8), half[k])]

    def term(k, slot, part):
        return half_of(k, slot, part, xq, w)

    def gathered(k, slot, part):
        return half_of(k, slot, part, yq, gw)

    def buffer(k, part, q_ref, w_ref):
        return q_ref.at[part] if k == 0 else w_ref.at[k - 1, part]

    far = functools.partial(buffer, q_ref=far_q, w_ref=far_w)
    direct = functools.partial(buffer, q_ref=direct_q, w_ref=direct_w)
    joined = functools.partial(buffer, q_ref=joined_q, w_ref=joined_w)
    partial = functools.partial(buffer, q_ref=partial_q, w_ref=partial_w)

    def remote(src, dst, sems, k, i, target):
        return pltpu.make_async_remote_copy(
            src_ref=src, dst_ref=dst, send_sem=sems[0].at[k, i], recv_sem=sems[1].at[k, i],
            device_id={"rep": target}, device_id_type=pl.DeviceIdType.MESH)

    def scatter_copies(k):
        sems = (rs_send, rs_recv)
        return (
            remote(term(k, across, 0), far(k, 0), sems, k, 0, after),
            remote(term(k, across, 1), far(k, 1), sems, k, 1, before),
            remote(term(k, after, 1), direct(k, 1), sems, k, 2, after),
            remote(term(k, before, 0), direct(k, 0), sems, k, 3, before),
            remote(partial(k, 0), joined(k, 0), sems, k, 4, after),
            remote(partial(k, 1), joined(k, 1), sems, k, 5, before),
        )

    scatter = [scatter_copies(k) for k in chunks]

    def scatter_start(k):
        for copy in scatter[k][:4]:
            copy.start()

    def scatter_relay(k):
        for i, target in enumerate((after, before)):
            scatter[k][i].wait_recv()
            partial(k, i)[...] = far(k, i)[...] + term(k, target, i)[...]
            scatter[k][4 + i].start()

    def scatter_finish(k):
        for copy in scatter[k][2:]:
            copy.wait_recv()
        sums = [term(k, me, i)[...] + direct(k, i)[...] + joined(k, i)[...] for i in range(2)]
        if k:
            send[k, pl.ds(0, half[k])] = sums[0]
            send[k, pl.ds(half[k], half[k])] = sums[1]
        else:
            full = jnp.concatenate(sums, 0)
            for g in range(groups):
                send[0, pl.ds(g, block, stride=groups)] = full[:, g].reshape(layers * width, block).T
        spread_start(send, got.at[k], 0, k, fw_send, fw_recv)

    def spread_start(src, dst, base, k, sem, other):
        n = share[k]

        def one(j, carry):
            target = lax.rem(own + j, shards)
            pltpu.make_async_remote_copy(
                src_ref=src.at[k, pl.ds(target * n, n)], dst_ref=dst.at[pl.ds(base + own * n, n)],
                send_sem=sem.at[k], recv_sem=other.at[k],
                device_id={"shard": target}, device_id_type=pl.DeviceIdType.MESH).start()
            return carry

        lax.fori_loop(1, shards, one, 0)
        pltpu.make_async_copy(src.at[k, pl.ds(own * n, n)], dst.at[pl.ds(base + own * n, n)], other.at[k]).start()

    def spread_sent(src, k, sem):
        part = src.at[k, pl.ds(0, (shards - 1) * share[k])]
        pltpu.make_async_copy(part, part, sem.at[k]).wait()

    def spread_arrived(dst, k, sem):
        pltpu.make_async_copy(dst, dst, sem.at[k]).wait()

    def to_rows(g):
        wi_loads[g].wait()
        for j in range(xw.shape[3] // LANES):
            tile = xw[g, :, :, pl.ds(j * LANES, LANES)].reshape(layers * width, LANES)
            w[g, pl.ds(j * LANES, LANES)] = tile.T

    def from_rows(g):
        for j in range(yw.shape[3] // LANES):
            tile = gw[g, pl.ds(j * LANES, LANES)].T
            yw[g, :, :, pl.ds(j * LANES, LANES)] = tile.reshape(layers, width, LANES)

    def own_qkv():
        spread_arrived(got.at[0, pl.ds(0, rows[0])], 0, fw_recv)
        n = share[0]
        masks = block_masks(share_q)
        for q in range(quads):
            lanes = pl.ds(q * LANES, LANES)
            for g in range(groups):
                four = [got[0, pl.ds((4 * q + j) * n + g, share_q, stride=groups)] for j in range(4)]
                for l, value in enumerate(swap_blocks(four, masks)):
                    dq[l, g, :, lanes] = value
        for l in range(layers):
            qm[l], qv[l] = outer_update(qm[l], qv[l], dq[l] / reps)
        for q in range(quads):
            lanes = pl.ds(q * LANES, LANES)
            for g in range(groups):
                four = swap_blocks([qm[l, g, :, lanes] for l in range(layers)], masks)
                for j, value in enumerate(four):
                    back[0, pl.ds((4 * q + j) * n + g, share_q, stride=groups)] = value
        spread_start(back, gq, 0, 0, bw_send, bw_recv)
        for copy in state_stores[:2]:
            copy.start()

    def own_wi(g):
        k, n = 1 + g, share_w
        spread_arrived(got.at[k, pl.ds(0, rows[k])], k, fw_recv)
        masks = block_masks(n)
        for q in range(quads):
            lanes = pl.ds(q * LANES, LANES)
            four = [got[k, pl.ds((4 * q + j) * n, n)] for j in range(4)]
            for l, value in enumerate(swap_blocks(four, masks)):
                dw[l, pl.ds(0, n), lanes] = value
        total = dw[...].reshape(-1, dw.shape[2])
        coef = lax.dot_general(total, basis[...], (((1,), (1,)), ((), ())), precision=lax.Precision.HIGHEST,
                               preferred_element_type=jnp.float32) / reps
        aw[...] = lax.dot_general(coef, basis[...], (((1,), (0,)), ((), ())), precision=lax.Precision.HIGHEST,
                                  preferred_element_type=jnp.float32).reshape(aw.shape)
        for l in range(layers):
            wm[g, l], wv[g, l] = outer_update(wm[g, l], wv[g, l], aw[l, pl.ds(0, n)])
        for q in range(quads):
            lanes = pl.ds(q * LANES, LANES)
            four = swap_blocks([wm[g, l, :, lanes] for l in range(layers)], masks)
            for j, value in enumerate(four):
                back[k, pl.ds((4 * q + j) * n, n)] = value
        spread_start(back, gw.at[g], me * rows[k], k, bw_send, bw_recv)
        for copy in state_stores[2 + 2 * g:4 + 2 * g]:
            copy.start()

    state_stores = [pltpu.make_async_copy(qm, qm_out, out_sem.at[0]), pltpu.make_async_copy(qv, qv_out, out_sem.at[1])]
    for g in range(2):
        state_stores += [pltpu.make_async_copy(wm.at[g], wm_out.at[:, :, g, :], out_sem.at[2 + g]),
                         pltpu.make_async_copy(wv.at[g], wv_out.at[:, :, g, :], out_sem.at[4 + g])]
    wt_stores = [pltpu.make_async_copy(yw.at[g], wt_out.at[:, :, g, :], out_sem.at[6 + g]) for g in range(2)]
    qt_stores = [pltpu.make_async_copy(yq.at[j], qt_out.at[:, :, :, pl.ds(j * block, block)], out_sem.at[8 + j])
                 for j in range(reps)]

    def gather_copies(k):
        def same(slot, part, i, target):
            there = gathered(k, slot, part)
            return remote(there, there, (ag_send, ag_recv), k, i, target)

        return (same(me, 0, 0, after), same(me, 1, 1, before),
                same(me, 1, 2, after), same(me, 0, 3, before),
                same(before, 0, 4, after), same(after, 1, 5, before))

    gather = [gather_copies(k) for k in chunks]

    def gather_start(k):
        if k:
            spread_arrived(gw.at[k - 1, pl.ds(pl.multiple_of(me * rows[k], 8), rows[k])], k, bw_recv)
        else:
            spread_arrived(gq, 0, bw_recv)
            for g in range(groups):
                tile = gq[pl.ds(g, block, stride=groups)].T
                yq[me, :, g] = tile.reshape(layers, width, block)
        for copy in gather[k][:4]:
            copy.start()

    def gather_relay(k):
        for i in range(2):
            gather[k][i].wait_recv()
            gather[k][4 + i].start()

    def gather_finish(k):
        for copy in gather[k][2:]:
            copy.wait_recv()
        if k:
            from_rows(k - 1)
            wt_stores[k - 1].start()
        else:
            for copy in qt_stores:
                copy.start()

    def wait_all(copies):
        for copy in copies:
            copy.wait()

    wait_all(loads)
    scatter_start(0)
    to_rows(0)
    scatter_start(1)
    scatter_relay(0)
    to_rows(1)
    scatter_start(2)
    scatter_relay(1)
    scatter_finish(0)
    scatter_relay(2)
    scatter_finish(1)
    wait_all(state_loads)
    own_qkv()
    scatter_finish(2)
    own_wi(0)
    gather_start(0)
    own_wi(1)
    gather_relay(0)
    gather_start(1)
    gather_relay(1)
    gather_finish(0)
    gather_start(2)
    gather_relay(2)
    gather_finish(1)
    gather_finish(2)
    for k in chunks:
        for copy in scatter[k] + gather[k]:
            copy.wait_send()
        spread_sent(send, k, fw_send)
        spread_sent(back, k, bw_send)
    wait_all(state_stores + wt_stores + qt_stores)


def per_device(qkv_delta, wi_delta, basis, qkv_master, qkv_momentum, wi_master, wi_momentum):
    reps, shards = lax.axis_size("rep"), lax.axis_size("shard")
    _, layers, width, groups, cols = qkv_delta.shape
    ff = wi_delta.shape[4]
    share_q, total = qkv_master.shape[3:]
    share_w = wi_master.shape[3]
    block = cols // reps
    tall = max(groups * share_q, share_w) * shards
    f32 = jnp.float32
    shape = functools.partial(jax.ShapeDtypeStruct, dtype=f32)
    vmem = lambda *dims: pltpu.VMEM(dims, f32)
    dma = pltpu.SemaphoreType.DMA
    anywhere = pl.BlockSpec(memory_space=pl.ANY)
    padded = -(-share_w // 8) * 8
    outs = pl.pallas_call(
        functools.partial(kernel, reps, shards),
        out_shape=(
            shape((layers, groups, share_q, total)), shape((layers, groups, share_q, total)),
            shape((layers, share_w, 2, total)), shape((layers, share_w, 2, total)),
            shape((layers, groups, width, cols)), shape((layers, width, 2, ff)),
        ),
        in_specs=[anywhere] * 7,
        out_specs=(anywhere,) * 6,
        scratch_shapes=[
            vmem(reps, layers, groups, width, block),
            vmem(2, layers, width, ff),
            vmem(2, ff, LANES),
            *[vmem(2, layers // 2, groups, width, block)] * 4,
            *[vmem(2, 2, ff // reps // 2, LANES)] * 4,
            vmem(3, tall, LANES), vmem(3, tall, LANES), vmem(3, tall, LANES),
            vmem(groups * share_q * shards, LANES),
            vmem(reps, layers, groups, width, block),
            vmem(2, ff, LANES),
            vmem(2, layers, width, ff),
            vmem(layers, groups, share_q, total),
            vmem(layers, padded, total), vmem(layers, padded, total),
            vmem(basis.shape[1], total),
            vmem(layers, groups, share_q, total), vmem(layers, groups, share_q, total),
            vmem(2, layers, share_w, total), vmem(2, layers, share_w, total),
            dma((3, 6)), dma((3, 6)), dma((3, 6)), dma((3, 6)),
            dma((3,)), dma((3,)), dma((3,)), dma((3,)),
            dma((10 + reps,)), dma((8 + reps,)),
        ],
        compiler_params=pltpu.CompilerParams(
            collective_id=0, has_side_effects=True, vmem_limit_bytes=48 * 2**20
        ),
    )(
        jnp.transpose(qkv_delta[0], (0, 2, 1, 3)), wi_delta[0], basis.T, qkv_master[0], qkv_momentum[0],
        jnp.transpose(wi_master[0], (0, 2, 1, 3)), jnp.transpose(wi_momentum[0], (0, 2, 1, 3)),
    )
    qm, qv, wm, wv, qt, wt = outs
    return (qm[None], qv[None], jnp.transpose(wm, (0, 2, 1, 3))[None], jnp.transpose(wv, (0, 2, 1, 3))[None],
            jnp.transpose(qt, (0, 2, 1, 3)), wt)


def solution(mesh):
    delta = P("rep", None, "shard", None, "tp")
    state = P("tp", None, None, ("rep", "shard"), None)
    train = P(None, "shard", None, "tp")
    return jax.shard_map(
        per_device, mesh=mesh, in_specs=(delta, delta, P(), state, state, state, state),
        out_specs=(state, state, state, state, train, train), check_vma=False,
    )
```

time: 1510 us -> 75.1 us (0.05)
  waiting for transfers between devices: 1380 us -> 0 us
  Pallas kernels: 0 us -> 63.1 us
  local copies, waits for them, and re-layouts: 68.7 us -> 10.7 us
  starting transfers between devices: 22.7 us -> 0 us
    unnamed x5 -> x0, waiting for transfers between devices: 1330 us -> none
    pallas_call x0 -> x1, Pallas kernels: none -> 63.1 us  [per_device(): pl.pallas_call(functools.partial(kernel, reps, shards), out_shape=(shape(...]
    all_to_all x3 -> x0, waiting for transfers between devices: 45.3 us -> none  [the longest x1 29 us: per_device(): lax.all_to_all(wi_stacked, 'shard', split_axis=3, concat_axis=3, tiled=True)]
    all_to_all x3 -> x0, starting transfers between devices: 22.6 us -> none  [the longest x1 9.91 us: per_device(): lax.all_to_all(summed, 'shard', split_axis=3, concat_axis=3, tiled=True)]
  transfers between devices with their start and end apart: 6 -> 0, of which waited for: 5 -> 0; matrix products, arithmetic and copies ran while one was open for 3% -> 0% of each run, Pallas kernels for 0% -> 0%
where the time goes in v1:
time: 75.1 us; the launch traced here: 74.4 us
  Pallas kernels  63.1 us (84%)
  local copies, waits for them, and re-layouts  10.7 us (14%)
    pallas_call x1, Pallas kernels, per_device(): pl.pallas_call(functools.partial(kernel, reps, shards), out_shape=(shape(...  63.1 us
    unnamed x18, local copies, waits for them, and re-layouts  10.7 us

profile of v1, /device:TPU:1, one launch (start us, length us, event | category | flops | bytes accessed | tf_op | source)
XLA Modules:
  0.0 74.4 jit_solution(2876202305809428176)
XLA Ops:
  0.6 0.0 copy-start
  0.6 1.1 %copy-done = f32[1,4,32,3,512]{4,2,3,1,0:T(8,128)S(1)} copy-done((f32[1,4,32,3,512]{4,2,3,1,0:T(8,128)S(1)}, f32[1,4,32,3,512]{4,2,3,1,0:T(8,128)}, u32[]{:S(2)}) %copy-start) | copy-done | bytes 786456
  1.8 0.0 copy-start.1
  1.8 1.0 %copy-done.1 = f32[1,4,2,11,1024]{4,2,3,1,0:T(2,128)S(1)} copy-done((f32[1,4,2,11,1024]{4,2,3,1,0:T(2,128)S(1)}, f32[1,4,2,11,1024]{4,2,3,1,0:T(2,128)}, u32[]{:S(2)}) %copy-start.1) | copy-done | bytes 360472
  2.8 0.0 copy-start.2
  2.8 1.0 %copy-done.2 = f32[1,4,2,11,1024]{4,2,3,1,0:T(2,128)S(1)} copy-done((f32[1,4,2,11,1024]{4,2,3,1,0:T(2,128)S(1)}, f32[1,4,2,11,1024]{4,2,3,1,0:T(2,128)}, u32[]{:S(2)}) %copy-start.2) | copy-done | bytes 360472
  3.7 0.0 copy-start.3
  3.7 0.9 %copy-done.3 = f32[1024,64]{0,1:T(8,128)S(1)} copy-done((f32[1024,64]{0,1:T(8,128)S(1)}, f32[1024,64]{0,1:T(8,128)}, u32[]{:S(2)}) %copy-start.3) | copy-done | bytes 262168
  4.7 0.0 copy-start.4
  4.7 0.9 %copy-done.4 = f32[1,4,3,4,1024]{4,3,2,1,0:T(4,128)S(1)} copy-done((f32[1,4,3,4,1024]{4,3,2,1,0:T(4,128)S(1)}, f32[1,4,3,4,1024]{4,3,2,1,0:T(4,128)}, u32[]{:S(2)}) %copy-start.4) | copy-done | bytes 196632
  5.6 0.0 copy-start.5
  5.6 0.9 %copy-done.5 = f32[1,4,3,4,1024]{4,3,2,1,0:T(4,128)S(1)} copy-done((f32[1,4,3,4,1024]{4,3,2,1,0:T(4,128)S(1)}, f32[1,4,3,4,1024]{4,3,2,1,0:T(4,128)}, u32[]{:S(2)}) %copy-start.5) | copy-done | bytes 196632
  6.5 63.1 %shard_map.118 = (f32[4,3,4,1024]{3,2,1,0:T(4,128)S(1)}, f32[4,3,4,1024]{3,2,1,0:T(4,128)S(1)}, f32[4,11,2,1024]{3,2,1,0:T(2,128)S(1)}, f32[4,11,2,1024]{3,2,1,0...) custom-call(f32[4,3,32,512]{3,2,1,0:T(8,128)S(1)} %bitcast.22, f32[4,32,2,1408]{3,2,1,0:T(2,128)} %bitcast.33, ...), custom_call_target="tpu_custom_call" | custom-call | tf_op jit(solution)/shard_map/pallas_call | solution.py:311
  69.6 0.7 copy.19
  70.3 0.7 copy.20
  71.0 0.7 copy.21
  71.7 0.7 copy.22
  72.4 0.9 %copy.23 = f32[4,32,3,512]{3,1,2,0:T(8,128)} copy(f32[4,32,3,512]{3,1,2,0:T(8,128)S(1)} %bitcast.23) | data formatting | bytes 1572864
  73.3 1.1 %copy.24 = f32[4,32,2,1408]{3,2,1,0:T(2,128)} copy(f32[4,32,2,1408]{3,2,1,0:T(2,128)S(1)} %get-tuple-element.29) | data formatting | bytes 2883584
Async XLA Ops:
  0.6 1.1 %copy-start = (f32[1,4,32,3,512]{4,2,3,1,0:T(8,128)S(1)}, f32[1,4,32,3,512]{4,2,3,1,0:T(8,128)}, u32[]{:S(2)}) copy-start(f32[1,4,32,3,512]{4,2,3,1,0:T(8,128)} %param.7) | copy-start | bytes 2359300
  1.8 1.0 %copy-start.1 = (f32[1,4,2,11,1024]{4,2,3,1,0:T(2,128)S(1)}, f32[1,4,2,11,1024]{4,2,3,1,0:T(2,128)}, u32[]{:S(2)}) copy-start(f32[1,4,2,11,1024]{4,2,3,1,0:T(2,128)} %param.12) | copy-start | bytes 1081348
  2.8 1.0 %copy-start.2 = (f32[1,4,2,11,1024]{4,2,3,1,0:T(2,128)S(1)}, f32[1,4,2,11,1024]{4,2,3,1,0:T(2,128)}, u32[]{:S(2)}) copy-start(f32[1,4,2,11,1024]{4,2,3,1,0:T(2,128)} %param.13) | copy-start | bytes 1081348
  3.7 0.9 %copy-start.3 = (f32[1024,64]{0,1:T(8,128)S(1)}, f32[1024,64]{0,1:T(8,128)}, u32[]{:S(2)}) copy-start(f32[1024,64]{0,1:T(8,128)} %param.9) | copy-start | bytes 786436
  4.7 0.9 %copy-start.4 = (f32[1,4,3,4,1024]{4,3,2,1,0:T(4,128)S(1)}, f32[1,4,3,4,1024]{4,3,2,1,0:T(4,128)}, u32[]{:S(2)}) copy-start(f32[1,4,3,4,1024]{4,3,2,1,0:T(4,128)} %param.10) | copy-start | bytes 589828
  5.6 0.9 %copy-start.5 = (f32[1,4,3,4,1024]{4,3,2,1,0:T(4,128)S(1)}, f32[1,4,3,4,1024]{4,3,2,1,0:T(4,128)}, u32[]{:S(2)}) copy-start(f32[1,4,3,4,1024]{4,3,2,1,0:T(4,128)} %param.11) | copy-start | bytes 589828

commit v2 on v1

--- a/solution.py
+++ b/solution.py
@@ -36,7 +36,7 @@
      xq, xw, w, far_q, direct_q, joined_q, partial_q, far_w, direct_w, joined_w, partial_w, send, got, back, gq, yq, gw, yw,
      dq, dw, aw, basis, qm, qv, wm, wv,
      rs_send, rs_recv, ag_send, ag_recv, fw_send, fw_recv, bw_send, bw_recv,
-     in_sem, out_sem) = refs
+     in_sem, out_sem, news) = refs
     layers, groups, width, block = xq.shape[1:]
     share_q, share_w = qm.shape[2], wm.shape[2]
     me = lax.axis_index("rep")
@@ -61,17 +61,58 @@
     for copy in loads + wi_loads + state_loads:
         copy.start()
 
+    cores, line = 2, min(4, shards // 2)
+    ring = shards // (cores * line)
+    core = lax.rem(own, cores)
+    spot = lax.rem(lax.div(own, cores), line)
+    partner = own + 1 - 2 * core
+    up, down = own + cores, own - cores
+    has_up, has_down = spot < line - 1, spot > 0
+    stride = cores * line
+    forth = lax.rem(own + stride, shards)
+    aback = lax.rem(own + shards - stride, shards)
+
+    def tell(sem, **target):
+        pl.semaphore_signal(sem, inc=1, device_id=target)
+
     barrier = pltpu.get_barrier_semaphore()
-    for target in (after, before):
-        pl.semaphore_signal(barrier, inc=1, device_id={"rep": target})
-
-    def greet(j, carry):
-        pl.semaphore_signal(barrier, inc=1, device_id={"shard": lax.rem(own + j, shards)})
-        return carry
-
-    lax.fori_loop(1, shards, greet, 0)
+    tell(barrier, rep=after)
+    tell(barrier, rep=before)
+    tell(barrier, shard=partner)
+    if ring > 1:
+        tell(barrier, shard=forth)
+        tell(barrier, shard=aback)
+    pl.when(has_up)(lambda: tell(barrier, shard=up))
+    pl.when(has_down)(lambda: tell(barrier, shard=down))
     dw[...] = jnp.zeros_like(dw)
-    pl.semaphore_wait(barrier, shards + 1)
+    near = 3 + (2 if ring > 1 else 0)
+    pl.semaphore_wait(barrier, near + has_up.astype(jnp.int32) + has_down.astype(jnp.int32))
+
+    def hear_line():
+        @pl.when(has_down)
+        def _():
+            pl.semaphore_wait(news.at[0], 1)
+
+        pl.when(has_up)(lambda: tell(news.at[0], shard=up))
+
+        @pl.when(has_up)
+        def _():
+            pl.semaphore_wait(news.at[1], 1)
+
+        pl.when(has_down)(lambda: tell(news.at[1], shard=down))
+
+    def hear_ring():
+        if ring > 1:
+            tell(news.at[2], shard=forth)
+            tell(news.at[3], shard=aback)
+            pl.semaphore_wait(news.at[2], 1)
+            tell(news.at[4], shard=forth)
+            pl.semaphore_wait(news.at[3], 1)
+            pl.semaphore_wait(news.at[4], 1)
+        tell(news.at[5], shard=partner)
+
+    def hear_partner():
+        pl.semaphore_wait(news.at[5], 1)
 
     def half_of(k, slot, part, q_ref, w_ref):
         if k == 0:
@@ -214,10 +255,10 @@
 
     state_stores = [pltpu.make_async_copy(qm, qm_out, out_sem.at[0]), pltpu.make_async_copy(qv, qv_out, out_sem.at[1])]
     for g in range(2):
-        state_stores += [pltpu.make_async_copy(wm.at[g], wm_out.at[:, :, g, :], out_sem.at[2 + g]),
-                         pltpu.make_async_copy(wv.at[g], wv_out.at[:, :, g, :], out_sem.at[4 + g])]
-    wt_stores = [pltpu.make_async_copy(yw.at[g], wt_out.at[:, :, g, :], out_sem.at[6 + g]) for g in range(2)]
-    qt_stores = [pltpu.make_async_copy(yq.at[j], qt_out.at[:, :, :, pl.ds(j * block, block)], out_sem.at[8 + j])
+        state_stores += [pltpu.make_async_copy(wm.at[g], wm_out.at[g], out_sem.at[2 + g]),
+                         pltpu.make_async_copy(wv.at[g], wv_out.at[g], out_sem.at[4 + g])]
+    wt_stores = [pltpu.make_async_copy(yw.at[g], wt_out.at[g], out_sem.at[6 + g]) for g in range(2)]
+    qt_stores = [pltpu.make_async_copy(yq.at[j], qt_out.at[j], out_sem.at[8 + j])
                  for j in range(reps)]
 
     def gather_copies(k):
@@ -266,9 +307,12 @@
     to_rows(0)
     scatter_start(1)
     scatter_relay(0)
+    hear_line()
     to_rows(1)
     scatter_start(2)
+    hear_ring()
     scatter_relay(1)
+    hear_partner()
     scatter_finish(0)
     scatter_relay(2)
     scatter_finish(1)
@@ -294,6 +338,20 @@
     wait_all(state_stores + wt_stores + qt_stores)
 
 
+def write_out(qm, qv, wm, wv, yq, yw, qm_out, qv_out, wm_out, wv_out, qt_out, wt_out, sem):
+    reps, block = yq.shape[0], yq.shape[4]
+    copies = [(qm, qm_out), (qv, qv_out)]
+    for g in range(2):
+        copies += [(wm.at[g], wm_out.at[:, :, g, :]), (wv.at[g], wv_out.at[:, :, g, :]),
+                   (yw.at[g], wt_out.at[:, :, g, :])]
+    copies += [(yq.at[j], qt_out.at[:, :, :, pl.ds(j * block, block)]) for j in range(reps)]
+    copies = [pltpu.make_async_copy(src, dst, sem.at[i]) for i, (src, dst) in enumerate(copies)]
+    for copy in copies:
+        copy.start()
+    for copy in copies:
+        copy.wait()
+
+
 def per_device(qkv_delta, wi_delta, basis, qkv_master, qkv_momentum, wi_master, wi_momentum):
     reps, shards = lax.axis_size("rep"), lax.axis_size("shard")
     _, layers, width, groups, cols = qkv_delta.shape
@@ -312,10 +370,10 @@
         functools.partial(kernel, reps, shards),
         out_shape=(
             shape((layers, groups, share_q, total)), shape((layers, groups, share_q, total)),
-            shape((layers, share_w, 2, total)), shape((layers, share_w, 2, total)),
-            shape((layers, groups, width, cols)), shape((layers, width, 2, ff)),
+            shape((2, layers, share_w, total)), shape((2, layers, share_w, total)),
+            shape((reps, layers, groups, width, block)), shape((2, layers, width, ff)),
         ),
-        in_specs=[anywhere] * 7,
+        in_specs=[pl.BlockSpec(memory_space=pltpu.HBM)] * 7,
         out_specs=(anywhere,) * 6,
         scratch_shapes=[
             vmem(reps, layers, groups, width, block),
@@ -335,16 +393,27 @@
             vmem(2, layers, share_w, total), vmem(2, layers, share_w, total),
             dma((3, 6)), dma((3, 6)), dma((3, 6)), dma((3, 6)),
             dma((3,)), dma((3,)), dma((3,)), dma((3,)),
-            dma((10 + reps,)), dma((8 + reps,)),
+            dma((10 + reps,)), dma((8 + reps,)), pltpu.SemaphoreType.REGULAR((6,)),
         ],
         compiler_params=pltpu.CompilerParams(
             collective_id=0, has_side_effects=True, vmem_limit_bytes=48 * 2**20
         ),
-    )(
+    )(*(pltpu.with_memory_space_constraint(x, pltpu.HBM) for x in (
         jnp.transpose(qkv_delta[0], (0, 2, 1, 3)), wi_delta[0], basis.T, qkv_master[0], qkv_momentum[0],
         jnp.transpose(wi_master[0], (0, 2, 1, 3)), jnp.transpose(wi_momentum[0], (0, 2, 1, 3)),
-    )
-    qm, qv, wm, wv, qt, wt = outs
+    )))
+    qm, qv, wm, wv, qt, wt = pl.pallas_call(
+        write_out,
+        out_shape=(
+            shape((layers, groups, share_q, total)), shape((layers, groups, share_q, total)),
+            shape((layers, share_w, 2, total)), shape((layers, share_w, 2, total)),
+            shape((layers, groups, width, cols)), shape((layers, width, 2, ff)),
+        ),
+        in_specs=[anywhere] * 6,
+        out_specs=(anywhere,) * 6,
+        scratch_shapes=[dma((8 + reps,))],
+        compiler_params=pltpu.CompilerParams(vmem_limit_bytes=2**17),
+    )(*outs)
     return (qm[None], qv[None], jnp.transpose(wm, (0, 2, 1, 3))[None], jnp.transpose(wv, (0, 2, 1, 3))[None],
             jnp.transpose(qt, (0, 2, 1, 3)), wt)
 

time: 75.1 us -> 63.9 us (0.85)
  local copies, waits for them, and re-layouts: 10.7 us -> 0 us
    unnamed x18 -> x0, local copies, waits for them, and re-layouts: 10.7 us -> none
    pallas_call x1, Pallas kernels: 63.1 us -> 60.7 us  [per_device(): pl.pallas_call(functools.partial(kernel, reps, shards), out_shape=(shape(...]
    pallas_call x0 -> x1, Pallas kernels: none -> 1.82 us  [per_device(): pl.pallas_call(write_out, out_shape=(shape((layers, groups, share_q, tota...]
where the time goes in v2:
time: 63.9 us; the launch traced here: 63.2 us
  Pallas kernels  62.5 us (98%)
  between operations  0.64 us (1%)
    pallas_call x1, Pallas kernels, per_device(): pl.pallas_call(functools.partial(kernel, reps, shards), out_shape=(shape(...  60.7 us
    pallas_call x1, Pallas kernels, per_device(): pl.pallas_call(write_out, out_shape=(shape((layers, groups, share_q, tota...  1.82 us

profile of v2, /device:TPU:1, one launch (start us, length us, event | category | flops | bytes accessed | tf_op | source)
XLA Modules:
  0.0 63.2 jit_solution(1626445616627002275)
XLA Ops:
  0.6 60.7 %shard_map.118 = (f32[4,3,4,1024]{3,2,1,0:T(4,128)S(1)}, f32[4,3,4,1024]{3,2,1,0:T(4,128)S(1)}, f32[2,4,11,1024]{3,2,1,0:T(8,128)S(1)}, f32[2,4,11,1024]{3,2,1,0...) custom-call(f32[4,3,32,512]{3,2,1,0:T(8,128)} %bitcast.23, f32[4,32,2,1408]{3,2,1,0:T(2,128)} %bitcast.22, ...), custom_call_target="tpu_custom_call" | custom-call | tf_op jit(solution)/shard_map/pallas_call | solution.py:369
  61.4 1.8 %shard_map.119 = (f32[4,3,4,1024]{3,2,1,0:T(4,128)}, f32[4,3,4,1024]{3,2,1,0:T(4,128)}, f32[4,11,2,1024]{3,2,1,0:T(2,128)}, f32[4,11,2,1024]{3,2,1,0:T(2,128)}, ...) custom-call(f32[4,3,4,1024]{3,2,1,0:T(4,128)S(1)} %get-tuple-element.18.qm, ...), custom_call_target="tpu_custom_call" | custom-call | tf_op jit(solution)/shard_map/pallas_call | solution.py:405

commit v3 on v2

v3 whole, which is shorter than its diff:
```python
import functools

import jax
import jax.numpy as jnp
from jax import lax
from jax.experimental import pallas as pl
from jax.experimental.pallas import tpu as pltpu
from jax.sharding import PartitionSpec as P

LANES = 128


def swap_blocks(four, masks):
    low_half, even = masks
    a, b, c, d = four
    a, c = jnp.where(low_half, a, pltpu.roll(c, 64, 1)), jnp.where(low_half, pltpu.roll(a, 64, 1), c)
    b, d = jnp.where(low_half, b, pltpu.roll(d, 64, 1)), jnp.where(low_half, pltpu.roll(b, 64, 1), d)
    a, b = jnp.where(even, a, pltpu.roll(b, 32, 1)), jnp.where(even, pltpu.roll(a, 96, 1), b)
    c, d = jnp.where(even, c, pltpu.roll(d, 32, 1)), jnp.where(even, pltpu.roll(c, 96, 1), d)
    return a, b, c, d


def block_masks(rows):
    lane = lax.broadcasted_iota(jnp.int32, (rows, LANES), 1)
    return lane < 64, lax.rem(lax.div(lane, 32), 2) == 0


def chunk_rows(chunk, share_q, share_w):
    return share_q if chunk[0] == "q" else share_w


def outer_update(master, momentum, average):
    momentum_new = 0.9 * momentum + average
    return master - 0.7 * (average + 0.9 * momentum_new), momentum_new


MOMENTUM = 0.7 * 0.9 * 0.9
AVERAGE = 0.7 * 1.9
CHUNKS = (("w", 0), ("w", 1), ("q", 0))


def kernel(reps, shards, chunks, *refs):
    refs = list(refs)

    def take(n):
        taken = refs[:n]
        del refs[:n]
        return taken

    qkv_in, wi_in, basis_in, qm_in, qv_in, wm_in, wv_in = take(7)
    qm_out, qv_out, wm_out, wv_out, qt_out, wt_out = take(6)
    far, direct, joined, partial, send, got, back, held, formed = (take(len(chunks)) for _ in range(9))
    xq, xw, yq, yw, dq, dw, aw, basis, qm, qv, wm, wv = take(12)
    rs_send, rs_recv, ag_send, ag_recv, fw_send, fw_recv, bw_send, bw_recv, in_sem, out_sem, news = refs
    layers, groups, width, block = xq.shape[1:]
    share_q, share_w = qm.shape[2], wm.shape[2]
    me = lax.axis_index("rep")
    own = lax.axis_index("shard")
    after = lax.rem(me + 1, reps)
    before = lax.rem(me + reps - 1, reps)
    across = lax.rem(me + 2, reps)
    quads = shards // 4
    share = tuple(chunk_rows(chunk, groups * share_q, share_w) for chunk in chunks)
    rows = tuple(shards * n for n in share)
    half = tuple(n // 2 for n in rows)

    loads = [pltpu.make_async_copy(qkv_in.at[:, :, :, pl.ds(j * block, block)], xq.at[j], in_sem.at[10 + j])
             for j in range(reps)]
    wi_loads = [pltpu.make_async_copy(wi_in.at[:, :, g, :], xw.at[g], in_sem.at[1 + g]) for g in range(2)]
    state_loads = [pltpu.make_async_copy(qm_in, qm, in_sem.at[3]), pltpu.make_async_copy(qv_in, qv, in_sem.at[4]),
                   pltpu.make_async_copy(basis_in, basis, in_sem.at[5])]
    for g in range(2):
        state_loads += [pltpu.make_async_copy(wm_in.at[:, :, g, :], wm.at[g], in_sem.at[6 + g]),
                        pltpu.make_async_copy(wv_in.at[:, :, g, :], wv.at[g], in_sem.at[8 + g])]
    for copy in loads + wi_loads + state_loads:
        copy.start()

    cores, line = 2, min(4, shards // 2)
    ring = shards // (cores * line)
    core = lax.rem(own, cores)
    spot = lax.rem(lax.div(own, cores), line)
    partner = own + 1 - 2 * core
    up, down = own + cores, own - cores
    has_up, has_down = spot < line - 1, spot > 0
    stride = cores * line
    forth = lax.rem(own + stride, shards)
    aback = lax.rem(own + shards - stride, shards)

    def tell(sem, **target):
        pl.semaphore_signal(sem, inc=1, device_id=target)

    barrier = pltpu.get_barrier_semaphore()
    tell(barrier, rep=after)
    tell(barrier, rep=before)
    tell(barrier, shard=partner)
    if ring > 1:
        tell(barrier, shard=forth)
        tell(barrier, shard=aback)
    pl.when(has_up)(lambda: tell(barrier, shard=up))
    pl.when(has_down)(lambda: tell(barrier, shard=down))
    dw[...] = jnp.zeros_like(dw)
    near = 3 + (2 if ring > 1 else 0)
    pl.semaphore_wait(barrier, near + has_up.astype(jnp.int32) + has_down.astype(jnp.int32))

    def pass_on(slot, here, **target):
        pl.when(here)(lambda: tell(news.at[slot], **target))

    def hear(slot, here):
        @pl.when(here)
        def _():
            pl.semaphore_wait(news.at[slot], 1)

    second, third = spot >= 2, spot >= 3
    second_last, third_last = spot <= line - 3, spot <= line - 4

    def round_1():
        pass_on(0, jnp.logical_and(has_up, has_down), shard=up)
        pass_on(1, jnp.logical_and(has_up, has_down), shard=down)
        if ring > 1:
            tell(news.at[2], shard=forth)

    def round_2():
        hear(0, second)
        hear(1, second_last)
        pass_on(3, jnp.logical_and(has_up, second), shard=up)
        pass_on(4, jnp.logical_and(has_down, second_last), shard=down)
        if ring > 1:
            pl.semaphore_wait(news.at[2], 1)

    def round_3():
        hear(3, third)
        hear(4, third_last)
        for i in range(1, ring):
            tell(news.at[5], shard=lax.rem(own + i * stride, shards))

    def round_4():
        if ring > 1:
            pl.semaphore_wait(news.at[5], ring - 1)
        tell(news.at[6], shard=partner)

    def round_5():
        pl.semaphore_wait(news.at[6], 1)

    def half_of(k, slot, part, q_ref, w_refs):
        if chunks[k][0] == "q":
            return q_ref.at[slot, pl.ds(part * (layers // 2), layers // 2)]
        return w_refs[k].at[pl.ds(pl.multiple_of(slot * rows[k] + part * half[k], 8), half[k])]

    def term(k, slot, part):
        return half_of(k, slot, part, xq, formed)

    def gathered(k, slot, part):
        return half_of(k, slot, part, yq, held)

    def remote(src, dst, sems, k, i, target):
        return pltpu.make_async_remote_copy(
            src_ref=src, dst_ref=dst, send_sem=sems[0].at[k, i], recv_sem=sems[1].at[k, i],
            device_id={"rep": target}, device_id_type=pl.DeviceIdType.MESH)

    def scatter_copies(k):
        sems = (rs_send, rs_recv)
        return (
            remote(term(k, across, 0), far[k].at[0], sems, k, 0, after),
            remote(term(k, across, 1), far[k].at[1], sems, k, 1, before),
            remote(term(k, after, 1), direct[k].at[1], sems, k, 2, after),
            remote(term(k, before, 0), direct[k].at[0], sems, k, 3, before),
            remote(partial[k].at[0], joined[k].at[0], sems, k, 4, after),
            remote(partial[k].at[1], joined[k].at[1], sems, k, 5, before),
        )

    scatter = [scatter_copies(k) for k in range(len(chunks))]

    def scatter_start(k):
        for copy in scatter[k][:4]:
            copy.start()

    def scatter_relay(k):
        for i, target in enumerate((after, before)):
            scatter[k][i].wait_recv()
            partial[k][i] = far[k][i] + term(k, target, i)[...]
            scatter[k][4 + i].start()

    def scatter_finish(k):
        for copy in scatter[k][2:]:
            copy.wait_recv()
        sums = [term(k, me, i)[...] + direct[k][i] + joined[k][i] for i in range(2)]
        if chunks[k][0] == "w":
            send[k][pl.ds(0, half[k])] = sums[0]
            send[k][pl.ds(half[k], half[k])] = sums[1]
        else:
            full = jnp.concatenate(sums, 0)
            spread_arrived(held[k], k, bw_recv)
            for g in range(groups):
                early = held[k][every(g, block, groups)].T.reshape(layers, width, block)
                yq[me, :, g] = early - AVERAGE / reps * full[:, g]
            for copy in gather[k][:4]:
                copy.start()
            for g in range(groups):
                send[k][every(g, block, groups)] = full[:, g].reshape(layers * width, block).T
        spread_start(send[k], got[k], 0, k, fw_send, fw_recv)

    def spread_start(src, dst, base, k, sem, other):
        n = share[k]

        def one(j, carry):
            target = lax.rem(own + j, shards)
            pltpu.make_async_remote_copy(
                src_ref=src.at[pl.ds(target * n, n)], dst_ref=dst.at[pl.ds(base + own * n, n)],
                send_sem=sem.at[k], recv_sem=other.at[k],
                device_id={"shard": target}, device_id_type=pl.DeviceIdType.MESH).start()
            return carry

        lax.fori_loop(1, shards, one, 0)
        pltpu.make_async_copy(src.at[pl.ds(own * n, n)], dst.at[pl.ds(base + own * n, n)], other.at[k]).start()

    def spread_sent(src, k, sem):
        part = src.at[pl.ds(0, (shards - 1) * share[k])]
        pltpu.make_async_copy(part, part, sem.at[k]).wait()

    def spread_arrived(dst, k, sem):
        pltpu.make_async_copy(dst, dst, sem.at[k]).wait()

    def every(start, count, step):
        return pl.ds(start, count, stride=step) if step > 1 else pl.ds(start, count)

    def to_rows(k):
        g = chunks[k][1]
        wi_loads[g].wait()
        for j in range(xw.shape[3] // LANES):
            tile = xw[g, :, :, pl.ds(j * LANES, LANES)].reshape(layers * width, LANES)
            formed[k][pl.ds(j * LANES, LANES)] = tile.T

    def from_rows(k):
        for j in range(yw.shape[3] // LANES):
            tile = held[k][pl.ds(j * LANES, LANES)].T
            yw[chunks[k][1], :, :, pl.ds(j * LANES, LANES)] = tile.reshape(layers, width, LANES)

    def own_rows(k):
        (own_qkv if chunks[k][0] == "q" else own_wi)(k)

    def early_qkv(k):
        masks = block_masks(share_q)
        for l in range(layers):
            dq[l] = qm[l] - MOMENTUM * qv[l]
        for q in range(quads):
            lanes = pl.ds(q * LANES, LANES)
            for g in range(groups):
                four = swap_blocks([dq[l, g, :, lanes] for l in range(layers)], masks)
                for j, value in enumerate(four):
                    back[k][every((4 * q + j) * share[k] + g, share_q, groups)] = value
        spread_start(back[k], held[k], 0, k, bw_send, bw_recv)

    def own_qkv(k):
        spread_arrived(got[k], k, fw_recv)
        masks = block_masks(share_q)
        for q in range(quads):
            lanes = pl.ds(q * LANES, LANES)
            for g in range(groups):
                four = [got[k][every((4 * q + j) * share[k] + g, share_q, groups)] for j in range(4)]
                for l, value in enumerate(swap_blocks(four, masks)):
                    dq[l, g, :, lanes] = value
        for l in range(layers):
            qm[l], qv[l] = outer_update(qm[l], qv[l], dq[l] / reps)
        for copy in state_stores[:2]:
            copy.start()

    def own_wi(k):
        g, n = chunks[k][1], share_w
        spread_arrived(got[k], k, fw_recv)
        masks = block_masks(n)
        for q in range(quads):
            lanes = pl.ds(q * LANES, LANES)
            four = [got[k][pl.ds((4 * q + j) * n, n)] for j in range(4)]
            for l, value in enumerate(swap_blocks(four, masks)):
                dw[l, pl.ds(0, n), lanes] = value
        total = dw[...].reshape(-1, dw.shape[2])
        coef = lax.dot_general(total, basis[...], (((1,), (1,)), ((), ())), precision=lax.Precision.HIGHEST,
                               preferred_element_type=jnp.float32) / reps
        aw[...] = lax.dot_general(
            coef, basis[...], (((1,), (0,)), ((), ())), precision=lax.Precision.HIGHEST,
            preferred_element_type=jnp.float32).reshape(aw.shape)
        for l in range(layers):
            wm[g, l], wv[g, l] = outer_update(wm[g, l], wv[g, l], aw[l, pl.ds(0, n)])
        for q in range(quads):
            lanes = pl.ds(q * LANES, LANES)
            four = swap_blocks([wm[g, l, :, lanes] for l in range(layers)], masks)
            for j, value in enumerate(four):
                back[k][pl.ds((4 * q + j) * n, n)] = value
        spread_start(back[k], held[k], me * rows[k], k, bw_send, bw_recv)
        for copy in state_stores[2 + 2 * g:4 + 2 * g]:
            copy.start()

    state_stores = [pltpu.make_async_copy(qm, qm_out, out_sem.at[0]), pltpu.make_async_copy(qv, qv_out, out_sem.at[1])]
    for g in range(2):
        state_stores += [pltpu.make_async_copy(wm.at[g], wm_out.at[g], out_sem.at[2 + g]),
                         pltpu.make_async_copy(wv.at[g], wv_out.at[g], out_sem.at[4 + g])]
    wt_stores = [pltpu.make_async_copy(yw.at[g], wt_out.at[g], out_sem.at[6 + g]) for g in range(2)]
    qt_stores = [pltpu.make_async_copy(yq.at[j], qt_out.at[j], out_sem.at[8 + j])
                 for j in range(reps)]

    def gather_copies(k):
        def same(slot, part, i, target):
            there = gathered(k, slot, part)
            return remote(there, there, (ag_send, ag_recv), k, i, target)

        return (same(me, 0, 0, after), same(me, 1, 1, before),
                same(me, 1, 2, after), same(me, 0, 3, before),
                same(before, 0, 4, after), same(after, 1, 5, before))

    gather = [gather_copies(k) for k in range(len(chunks))]

    def gather_start(k):
        spread_arrived(held[k].at[pl.ds(pl.multiple_of(me * rows[k], 8), rows[k])], k, bw_recv)
        for copy in gather[k][:4]:
            copy.start()

    def gather_relay(k):
        for i in range(2):
            gather[k][i].wait_recv()
            gather[k][4 + i].start()

    def gather_finish(k):
        for copy in gather[k][2:]:
            copy.wait_recv()
        if chunks[k][0] == "w":
            from_rows(k)
            wt_stores[chunks[k][1]].start()
        else:
            for copy in qt_stores:
                copy.start()

    def wait_all(copies):
        for copy in copies:
            copy.wait()

    wait_all(loads)
    to_rows(0)
    scatter_start(0)
    round_1()
    to_rows(1)
    round_2()
    scatter_relay(0)
    scatter_start(1)
    round_3()
    round_4()
    round_5()
    wait_all(state_loads)
    early_qkv(2)
    scatter_finish(0)
    scatter_relay(1)
    scatter_start(2)
    scatter_finish(1)
    scatter_relay(2)
    own_rows(0)
    scatter_finish(2)
    own_rows(1)
    gather_relay(2)
    gather_start(0)
    own_rows(2)
    gather_relay(0)
    gather_start(1)
    gather_finish(2)
    gather_finish(0)
    gather_relay(1)
    gather_finish(1)
    for k in range(len(chunks)):
        for copy in scatter[k] + gather[k]:
            copy.wait_send()
        spread_sent(send[k], k, fw_send)
        spread_sent(back[k], k, bw_send)
    wait_all(state_stores + wt_stores + qt_stores)


def write_out(qm, qv, wm, wv, yq, yw, qm_out, qv_out, wm_out, wv_out, qt_out, wt_out, sem):
    reps, block = yq.shape[0], yq.shape[4]
    copies = [(qm, qm_out), (qv, qv_out)]
    for g in range(2):
        copies += [(wm.at[g], wm_out.at[:, :, g, :]), (wv.at[g], wv_out.at[:, :, g, :]),
                   (yw.at[g], wt_out.at[:, :, g, :])]
    copies += [(yq.at[j], qt_out.at[:, :, :, pl.ds(j * block, block)]) for j in range(reps)]
    copies = [pltpu.make_async_copy(src, dst, sem.at[i]) for i, (src, dst) in enumerate(copies)]
    for copy in copies:
        copy.start()
    for copy in copies:
        copy.wait()


def per_device(qkv_delta, wi_delta, basis, qkv_master, qkv_momentum, wi_master, wi_momentum):
    reps, shards = lax.axis_size("rep"), lax.axis_size("shard")
    _, layers, width, groups, cols = qkv_delta.shape
    ff = wi_delta.shape[4]
    share_q, total = qkv_master.shape[3:]
    share_w = wi_master.shape[3]
    block = cols // reps
    chunks = CHUNKS
    sizes = [chunk_rows(chunk, groups * share_q, share_w) * shards for chunk in chunks]
    wide = [chunk[0] == "w" for chunk in chunks]
    f32 = jnp.float32
    shape = functools.partial(jax.ShapeDtypeStruct, dtype=f32)
    vmem = lambda *dims: pltpu.VMEM(dims, f32)
    dma = pltpu.SemaphoreType.DMA
    anywhere = pl.BlockSpec(memory_space=pl.ANY)
    padded = -(-share_w // 8) * 8
    outs = pl.pallas_call(
        functools.partial(kernel, reps, shards, chunks),
        out_shape=(
            shape((layers, groups, share_q, total)), shape((layers, groups, share_q, total)),
            shape((2, layers, share_w, total)), shape((2, layers, share_w, total)),
            shape((reps, layers, groups, width, block)), shape((2, layers, width, ff)),
        ),
        in_specs=[pl.BlockSpec(memory_space=pltpu.HBM)] * 7,
        out_specs=(anywhere,) * 6,
        scratch_shapes=[
            *[vmem(2, n // 2, LANES) if wi else vmem(2, layers // 2, groups, width, block)
              for n, wi in zip(sizes, wide)] * 4,
            *[vmem(n, LANES) for n in sizes] * 3,
            *[vmem(reps * n if wi else n, LANES) for n, wi in zip(sizes, wide)],
            *[vmem(reps * n if wi else 8, LANES) for n, wi in zip(sizes, wide)],
            vmem(reps, layers, groups, width, block), vmem(2, layers, width, ff),
            vmem(reps, layers, groups, width, block), vmem(2, layers, width, ff),
            vmem(layers, groups, share_q, total),
            vmem(layers, padded, total), vmem(layers, padded, total),
            vmem(basis.shape[1], total),
            vmem(layers, groups, share_q, total), vmem(layers, groups, share_q, total),
            vmem(2, layers, share_w, total), vmem(2, layers, share_w, total),
            *[dma((len(chunks), 6))] * 4, *[dma((len(chunks),))] * 4,
            dma((10 + reps,)), dma((8 + reps,)), pltpu.SemaphoreType.REGULAR((7,)),
        ],
        compiler_params=pltpu.CompilerParams(
            collective_id=0, has_side_effects=True, vmem_limit_bytes=48 * 2**20
        ),
    )(*(pltpu.with_memory_space_constraint(x, pltpu.HBM) for x in (
        jnp.transpose(qkv_delta[0], (0, 2, 1, 3)), wi_delta[0], basis.T, qkv_master[0], qkv_momentum[0],
        jnp.transpose(wi_master[0], (0, 2, 1, 3)), jnp.transpose(wi_momentum[0], (0, 2, 1, 3)),
    )))
    qm, qv, wm, wv, qt, wt = pl.pallas_call(
        write_out,
        out_shape=(
            shape((layers, groups, share_q, total)), shape((layers, groups, share_q, total)),
            shape((layers, share_w, 2, total)), shape((layers, share_w, 2, total)),
            shape((layers, groups, width, cols)), shape((layers, width, 2, ff)),
        ),
        in_specs=[anywhere] * 6,
        out_specs=(anywhere,) * 6,
        scratch_shapes=[dma((8 + reps,))],
        compiler_params=pltpu.CompilerParams(vmem_limit_bytes=2**17),
    )(*outs)
    return (qm[None], qv[None], jnp.transpose(wm, (0, 2, 1, 3))[None], jnp.transpose(wv, (0, 2, 1, 3))[None],
            jnp.transpose(qt, (0, 2, 1, 3)), wt)


def solution(mesh):
    delta = P("rep", None, "shard", None, "tp")
    state = P("tp", None, None, ("rep", "shard"), None)
    train = P(None, "shard", None, "tp")
    return jax.shard_map(
        per_device, mesh=mesh, in_specs=(delta, delta, P(), state, state, state, state),
        out_specs=(state, state, state, state, train, train), check_vma=False,
    )
```

time: 63.9 us -> 55.3 us (0.87)
  Pallas kernels: 62.5 us -> 54.5 us
    pallas_call x1, Pallas kernels: 60.7 us -> 52.7 us  [per_device(): pl.pallas_call(functools.partial(kernel, reps, shards, chunks), out_shape...]
where the time goes in v3:
time: 55.3 us; the launch traced here: 55.2 us
  Pallas kernels  54.5 us (99%)
  between operations  0.64 us (1%)
    pallas_call x1, Pallas kernels, per_device(): pl.pallas_call(functools.partial(kernel, reps, shards, chunks), out_shape...  52.7 us
    pallas_call x1, Pallas kernels, per_device(): pl.pallas_call(write_out, out_shape=(shape((layers, groups, share_q, tota...  1.82 us

profile of v3, /device:TPU:1, one launch (start us, length us, event | category | flops | bytes accessed | tf_op | source)
XLA Modules:
  0.0 55.2 jit_solution(14847554062193434373)
XLA Ops:
  0.6 52.7 %shard_map.118 = (f32[4,3,4,1024]{3,2,1,0:T(4,128)S(1)}, f32[4,3,4,1024]{3,2,1,0:T(4,128)S(1)}, f32[2,4,11,1024]{3,2,1,0:T(8,128)S(1)}, f32[2,4,11,1024]{3,2,1,0...) custom-call(f32[4,3,32,512]{3,2,1,0:T(8,128)} %bitcast.23, f32[4,32,2,1408]{3,2,1,0:T(2,128)} %bitcast.22, ...), custom_call_target="tpu_custom_call" | custom-call | tf_op jit(solution)/shard_map/pallas_call | solution.py:404
  53.4 1.8 %shard_map.119 = (f32[4,3,4,1024]{3,2,1,0:T(4,128)}, f32[4,3,4,1024]{3,2,1,0:T(4,128)}, f32[4,11,2,1024]{3,2,1,0:T(2,128)}, f32[4,11,2,1024]{3,2,1,0:T(2,128)}, ...) custom-call(f32[4,3,4,1024]{3,2,1,0:T(4,128)S(1)} %get-tuple-element.18.qm, ...), custom_call_target="tpu_custom_call" | custom-call | tf_op jit(solution)/shard_map/pallas_call | solution.py:436

commit v4 on v3

--- a/solution.py
+++ b/solution.py
@@ -64,17 +64,6 @@
     rows = tuple(shards * n for n in share)
     half = tuple(n // 2 for n in rows)
 
-    loads = [pltpu.make_async_copy(qkv_in.at[:, :, :, pl.ds(j * block, block)], xq.at[j], in_sem.at[10 + j])
-             for j in range(reps)]
-    wi_loads = [pltpu.make_async_copy(wi_in.at[:, :, g, :], xw.at[g], in_sem.at[1 + g]) for g in range(2)]
-    state_loads = [pltpu.make_async_copy(qm_in, qm, in_sem.at[3]), pltpu.make_async_copy(qv_in, qv, in_sem.at[4]),
-                   pltpu.make_async_copy(basis_in, basis, in_sem.at[5])]
-    for g in range(2):
-        state_loads += [pltpu.make_async_copy(wm_in.at[:, :, g, :], wm.at[g], in_sem.at[6 + g]),
-                        pltpu.make_async_copy(wv_in.at[:, :, g, :], wv.at[g], in_sem.at[8 + g])]
-    for copy in loads + wi_loads + state_loads:
-        copy.start()
-
     cores, line = 2, min(4, shards // 2)
     ring = shards // (cores * line)
     core = lax.rem(own, cores)
@@ -98,9 +87,21 @@
         tell(barrier, shard=aback)
     pl.when(has_up)(lambda: tell(barrier, shard=up))
     pl.when(has_down)(lambda: tell(barrier, shard=down))
+    loads = [pltpu.make_async_copy(qkv_in.at[:, :, :, pl.ds(j * block, block)], xq.at[j], in_sem.at[10 + j])
+             for j in range(reps)]
+    wi_loads = [pltpu.make_async_copy(wi_in.at[:, :, g, :], xw.at[g], in_sem.at[1 + g]) for g in range(2)]
+    state_loads = [pltpu.make_async_copy(qm_in, qm, in_sem.at[3]), pltpu.make_async_copy(qv_in, qv, in_sem.at[4]),
+                   pltpu.make_async_copy(basis_in, basis, in_sem.at[5])]
+    for g in range(2):
+        state_loads += [pltpu.make_async_copy(wm_in.at[:, :, g, :], wm.at[g], in_sem.at[6 + g]),
+                        pltpu.make_async_copy(wv_in.at[:, :, g, :], wv.at[g], in_sem.at[8 + g])]
+    for copy in wi_loads + loads + state_loads:
+        copy.start()
+
     dw[...] = jnp.zeros_like(dw)
-    near = 3 + (2 if ring > 1 else 0)
-    pl.semaphore_wait(barrier, near + has_up.astype(jnp.int32) + has_down.astype(jnp.int32))
+    def enter():
+        near = 3 + (2 if ring > 1 else 0)
+        pl.semaphore_wait(barrier, near + has_up.astype(jnp.int32) + has_down.astype(jnp.int32))
 
     def pass_on(slot, here, **target):
         pl.when(here)(lambda: tell(news.at[slot], **target))
@@ -180,13 +181,17 @@
             partial[k][i] = far[k][i] + term(k, target, i)[...]
             scatter[k][4 + i].start()
 
+    def summed(k):
+        return [term(k, me, i)[...] + direct[k][i] + joined[k][i] for i in range(2)]
+
     def scatter_finish(k):
         for copy in scatter[k][2:]:
             copy.wait_recv()
-        sums = [term(k, me, i)[...] + direct[k][i] + joined[k][i] for i in range(2)]
+        sums = summed(k)
         if chunks[k][0] == "w":
             send[k][pl.ds(0, half[k])] = sums[0]
             send[k][pl.ds(half[k], half[k])] = sums[1]
+            spread_start(send[k], got[k], 0, k, fw_send, fw_recv)
         else:
             full = jnp.concatenate(sums, 0)
             spread_arrived(held[k], k, bw_recv)
@@ -195,22 +200,22 @@
                 yq[me, :, g] = early - AVERAGE / reps * full[:, g]
             for copy in gather[k][:4]:
                 copy.start()
-            for g in range(groups):
-                send[k][every(g, block, groups)] = full[:, g].reshape(layers * width, block).T
+
+    def spread_qkv(k):
+        full = jnp.concatenate(summed(k), 0)
+        for g in range(groups):
+            send[k][every(g, block, groups)] = full[:, g].reshape(layers * width, block).T
         spread_start(send[k], got[k], 0, k, fw_send, fw_recv)
 
     def spread_start(src, dst, base, k, sem, other):
         n = share[k]
 
-        def one(j, carry):
-            target = lax.rem(own + j, shards)
+        for step in sorted(range(1, shards), key=lambda step: (-min(step % stride, stride - step % stride), step)):
+            target = lax.rem(own + step, shards)
             pltpu.make_async_remote_copy(
                 src_ref=src.at[pl.ds(target * n, n)], dst_ref=dst.at[pl.ds(base + own * n, n)],
                 send_sem=sem.at[k], recv_sem=other.at[k],
                 device_id={"shard": target}, device_id_type=pl.DeviceIdType.MESH).start()
-            return carry
-
-        lax.fori_loop(1, shards, one, 0)
         pltpu.make_async_copy(src.at[pl.ds(own * n, n)], dst.at[pl.ds(base + own * n, n)], other.at[k]).start()
 
     def spread_sent(src, k, sem):
@@ -333,8 +338,8 @@
         for copy in copies:
             copy.wait()
 
-    wait_all(loads)
     to_rows(0)
+    enter()
     scatter_start(0)
     round_1()
     to_rows(1)
@@ -348,20 +353,22 @@
     early_qkv(2)
     scatter_finish(0)
     scatter_relay(1)
+    wait_all(loads)
     scatter_start(2)
     scatter_finish(1)
     scatter_relay(2)
     own_rows(0)
     scatter_finish(2)
     own_rows(1)
+    spread_qkv(2)
     gather_relay(2)
     gather_start(0)
-    own_rows(2)
     gather_relay(0)
     gather_start(1)
-    gather_finish(2)
     gather_finish(0)
     gather_relay(1)
+    gather_finish(2)
+    own_rows(2)
     gather_finish(1)
     for k in range(len(chunks)):
         for copy in scatter[k] + gather[k]:

time: 55.3 us -> 52.1 us (0.942)
  Pallas kernels: 54.5 us -> 50.8 us
    pallas_call x1, Pallas kernels: 52.7 us -> 49 us  [per_device(): pl.pallas_call(functools.partial(kernel, reps, shards, chunks), out_shape...]
where the time goes in v4:
time: 52.1 us; the launch traced here: 51.5 us
  Pallas kernels  50.8 us (98%)
  between operations  0.64 us (1%)
    pallas_call x1, Pallas kernels, per_device(): pl.pallas_call(functools.partial(kernel, reps, shards, chunks), out_shape...  49 us
    pallas_call x1, Pallas kernels, per_device(): pl.pallas_call(write_out, out_shape=(shape((layers, groups, share_q, tota...  1.82 us

profile of v4, /device:TPU:1, one launch (start us, length us, event | category | flops | bytes accessed | tf_op | source)
XLA Modules:
  0.0 51.5 jit_solution(6421291065788027542)
XLA Ops:
  0.6 49.0 %shard_map.118 = (f32[4,3,4,1024]{3,2,1,0:T(4,128)S(1)}, f32[4,3,4,1024]{3,2,1,0:T(4,128)S(1)}, f32[2,4,11,1024]{3,2,1,0:T(8,128)S(1)}, f32[2,4,11,1024]{3,2,1,0...) custom-call(f32[4,3,32,512]{3,2,1,0:T(8,128)} %bitcast.23, f32[4,32,2,1408]{3,2,1,0:T(2,128)} %bitcast.22, ...), custom_call_target="tpu_custom_call" | custom-call | tf_op jit(solution)/shard_map/pallas_call | solution.py:411
  49.7 1.8 %shard_map.119 = (f32[4,3,4,1024]{3,2,1,0:T(4,128)}, f32[4,3,4,1024]{3,2,1,0:T(4,128)}, f32[4,11,2,1024]{3,2,1,0:T(2,128)}, f32[4,11,2,1024]{3,2,1,0:T(2,128)}, ...) custom-call(f32[4,3,4,1024]{3,2,1,0:T(4,128)S(1)} %get-tuple-element.18.qm, ...), custom_call_target="tpu_custom_call" | custom-call | tf_op jit(solution)/shard_map/pallas_call | solution.py:443
